TPU v7x, 32 devices: a whole 2x2x4 slice. The times are simulated.
32 devices in a mesh: row: 4 (over z), mix: 8 (over y, x, core).
Axes of the slice: x: 2, y: 2, z: 4, core: 2. Of those that a mesh axis runs over, the one named last changes fastest.
Arguments:
- velocity: bfloat16 [64, 3, 8, 32, 128], P(None, None, 'mix', 'row'), may hold values from -6 to 6
- field_b: bfloat16 [64, 3, 8, 32, 128], P(None, None, 'mix', 'row'), may hold values from -6 to 6
- test_signs: int32 [384, 256], replicated, may hold values from 0 to 1
- row_signs: int32 [8, 32, 128], P('mix', 'row'), may hold values from 0 to 1
- sample_index: int32 [8, 4, 256], P('mix', 'row'), may hold values from 0 to 1023
Outputs:
- basis_rows: float32 [8, 4, 256, 256], P('mix', 'row')
- factor: float32 [256, 256], replicated
Inputs may be any that keep to these rules, and one draw needn't show every extreme that they name: test_signs entries are bits; the test matrix is 2 test_signs - 1. row_signs entries are bits; the sign is 2 row_signs - 1. `sample_index`: a point of the device's own block, p = x_local 128 + y; repeats may occur.
All inputs are finite; a program needn't handle non-finite values.
Results may differ from a plain program's by a relative error of at most 0.0021.
Values may be sent and summed in bfloat16 or wider, within the bound.
No kernel may reach another device: no remote copies, remote signals or barrier semaphores. Data moves between devices by JAX's collectives and lax.ppermute only.
A program may use at most 64 MiB of HBM per device.

v0:
```python
import math
import jax
import jax.numpy as jnp
from jax import lax
from jax.sharding import PartitionSpec as P


def swapped(block, axis, distance):
    count = lax.axis_size(axis)
    route = []
    for low in range(count):
        high = low | 1 << distance
        if high != low and high < count:
            route += [(low, high), (high, low)]
    return lax.ppermute(block, axis, route)


def padded(shard, sides, width):
    for axis, dim in sides:
        size, length = (lax.axis_size(axis), shard.shape[dim])
        up = [(i, (i + 1) % size) for i in range(size - 1)]
        down = [(j, i) for i, j in up]
        last = lax.slice_in_dim(shard, length - width, length, axis=dim)
        first = lax.slice_in_dim(shard, 0, width, axis=dim)
        before = lax.ppermute(last, axis, up)
        after = lax.ppermute(first, axis, down)
        shard = jnp.concatenate([before, shard, after], axis=dim)
    return shard


def curl_plane(stencil_slab):
    center = stencil_slab[:, :, 1]

    def along_x(component):
        return (center[:, component, 2:, 1:-1] - center[:, component, :-2, 1:-1]) * 0.5

    def along_y(component):
        return (center[:, component, 1:-1, 2:] - center[:, component, 1:-1, :-2]) * 0.5

    def along_z(component):
        return (
            stencil_slab[:, component, 2, 1:-1, 1:-1] - stencil_slab[:, component, 0, 1:-1, 1:-1]
        ) * 0.5

    current_x = along_y(2) - along_z(1)
    current_y = along_z(0) - along_x(2)
    current_z = along_x(1) - along_y(0)
    return jnp.stack([current_x, current_y, current_z], axis=1).astype(jnp.bfloat16)


def pair_mixing(signed, planes):
    my_index = lax.axis_index("mix")
    values = signed
    for level in range(planes.bit_length() - 1):
        partner = swapped(values, "mix", level)
        upper_bit = my_index // (1 << level) % 2
        values = jnp.where(upper_bit == 1, partner - values, values + partner)
    return values / math.sqrt(planes)


def upper_factor(gram_matrix):
    return jnp.linalg.cholesky(gram_matrix).T


def on_device(velocity, field_b, test_signs, row_signs, sample_index):
    snaps = field_b.shape[0]
    sketch_width = test_signs.shape[1]
    planes = lax.axis_size("mix")
    row_blocks = lax.axis_size("row")
    with_rims = padded(field_b, (("row", 3), ("mix", 2)), 1)
    stencil_slab = jnp.pad(with_rims.astype(jnp.float32), ((0, 0), (0, 0), (0, 0), (0, 0), (1, 1)))
    current = curl_plane(stencil_slab)
    snapshot = jnp.concatenate([velocity[:, :, 0], current], axis=1).reshape(6 * snaps, -1)
    test_matrix = (2 * test_signs - 1).astype(jnp.bfloat16)
    sketch = lax.dot_general(
        snapshot, test_matrix, (((0,), (0,)), ((), ())), preferred_element_type=jnp.float32
    ) * (1.0 / math.sqrt(6 * snaps))
    point_signs = (2 * row_signs - 1).astype(jnp.float32).reshape(-1)
    signed = sketch * point_signs[:, None]
    mixed_rows = pair_mixing(signed, planes)
    picked = jnp.take(mixed_rows, sample_index.reshape(-1), axis=0)
    picked_total = planes * row_blocks * picked.shape[0]
    local_gram = (
        jnp.dot(
            picked.T, picked, precision=lax.Precision.HIGHEST, preferred_element_type=jnp.float32
        )
        / picked_total
    )
    block_factor = upper_factor(lax.psum(local_gram, "mix"))
    every_factor = lax.all_gather(block_factor[None], "row", axis=0, tiled=True)
    stacked_gram = jnp.einsum(
        "bij,bil->jl", every_factor, every_factor, precision=lax.Precision.HIGHEST
    )
    factor = upper_factor(stacked_gram)
    solved = jax.scipy.linalg.solve_triangular(factor.T, picked.T, lower=True)
    basis_rows = solved.T.reshape(sample_index.shape + (sketch_width,))
    return (basis_rows, factor)


def solution(mesh):
    return jax.shard_map(
        on_device,
        mesh=mesh,
        in_specs=(
            P(None, None, "mix", "row", None),
            P(None, None, "mix", "row", None),
            P(),
            P("mix", "row", None),
            P("mix", "row", None),
        ),
        out_specs=(P("mix", "row", None, None), P()),
        check_vma=False,
    )
```

profile of v0, /device:TPU:0, one launch (start us, length us, event | category | flops | bytes accessed | tf_op | source)
XLA Modules:
  0.0 284.6 jit_solution(11077461579640509562)
XLA Ops:
  7.2 1.4 fusion.46
  8.6 4.9 %collective-permute-start = (bf16[64,3,1,1,128]{4,0,3,2,1:T(8,128)(2,1)S(1)}, bf16[64,3,1,1,128]{4,0,3,2,1:T(8,128)(2,1)S(1)}, u32[]{:S(2)}, u32[]{:S(2)}) collective-permute-start(bf16[64,3,1,1,128]{4,0,3,2,1:T(8,128)(2,1)S(1)} %copy.62), channel_id=1, source_target_pairs={{0,8},{8,16},{16,24},{1,9},{9,17},{17,25},{2,10},{10,18},{18,26},{... | collective-permute-start | bytes 147464 | tf_op jit(solution)/shard_map/ppermute | solution.py:25
  13.6 1.3 collective-permute-start.1
  15.3 1.1 constant_dynamic-update-slice_fusion.1
  16.4 3.2 %collective-permute-done.1 = bf16[64,3,1,1,128]{4,0,3,2,1:T(8,128)(2,1)S(1)} collective-permute-done((bf16[64,3,1,1,128]{4,0,3,2,1:T(8,128)(2,1)S(1)}, bf16[64,3,1,1,128]{4,0,3,2,1:T(8,128)(2,1)S(1)}, u32[]{:S(2)}, u32[]{:S(2)}) %collective-permute-start.1) | collective-permute-done | bytes 49184 | tf_op jit(solution)/shard_map/ppermute | solution.py:26
  19.6 1.3 collective-permute-start.3
  20.9 3.1 %collective-permute-start.2 = (bf16[64,3,1,10,128]{4,0,3,2,1:T(8,128)(2,1)S(1)}, bf16[64,3,1,10,128]{4,0,3,2,1:T(8,128)(2,1)S(1)}, u32[]{:S(2)}, u32[]{:S(2)}) collective-permute-start(bf16[64,3,1,10,128]{4,0,3,2,1:T(8,128)(2,1)S(1)} %constant_dynamic-update-slice_fusion), channel_id=1, source_target_pairs={{0,1},{1,2},{2,3},{3,4},{4,5},{5,6},{6,7},{8,9},{9,10},{10,11},{11... | collective-permute-start | bytes 1474568 | tf_op jit(solution)/shard_map/ppermute | solution.py:25
  28.0 6.6 %collective-permute-start.4 = (f32[1024,256]{1,0:T(8,128)S(1)}, f32[1024,256]{1,0:T(8,128)S(1)}, u32[]{:S(2)}, u32[]{:S(2)}) collective-permute-start(f32[1024,256]{1,0:T(8,128)S(1)} %convolution_multiply_fusion), channel_id=1, source_target_pairs={{0,1},{1,0},{2,3},{3,2},{4,5},{5,4},{6,7},{7,6},{8,9},{9,8},{10,11... | collective-permute-start | bytes 3145736 | tf_op jit(solution)/shard_map/ppermute | solution.py:15
  34.6 2.3 collective-permute-done.4
  37.0 2.8 collective-permute-start.5
  39.9 23.7 %collective-permute-done.5 = f32[1024,256]{1,0:T(8,128)S(1)} collective-permute-done((f32[1024,256]{1,0:T(8,128)S(1)}, f32[1024,256]{1,0:T(8,128)S(1)}, u32[]{:S(2)}, u32[]{:S(2)}) %collective-permute-start.5) | collective-permute-done | bytes 1048608 | tf_op jit(solution)/shard_map/ppermute | solution.py:15
  63.7 3.7 %collective-permute-start.6 = (f32[1024,256]{1,0:T(8,128)S(1)}, f32[1024,256]{1,0:T(8,128)S(1)}, u32[]{:S(2)}, u32[]{:S(2)}) collective-permute-start(f32[1024,256]{1,0:T(8,128)S(1)} %add_select_fusion), channel_id=1, source_target_pairs={{0,4},{4,0},{1,5},{5,1},{2,6},{6,2},{3,7},{7,3},{8,12},{12,8},{9,1... | collective-permute-start | bytes 3145736 | tf_op jit(solution)/shard_map/ppermute | solution.py:15
  67.5 22.6 %collective-permute-done.6 = f32[1024,256]{1,0:T(8,128)S(1)} collective-permute-done((f32[1024,256]{1,0:T(8,128)S(1)}, f32[1024,256]{1,0:T(8,128)S(1)}, u32[]{:S(2)}, u32[]{:S(2)}) %collective-permute-start.6) | collective-permute-done | bytes 1048608 | tf_op jit(solution)/shard_map/ppermute | solution.py:15
  90.2 1.0 gather_fusion
  91.3 1.1 convolution_multiply_fusion.1
  92.7 53.0 %all-reduce.4.cloned.1.call-done = f32[256,256]{0,1:T(8,128)} async-done(((f32[256,256]{0,1:T(8,128)}), f32[256,256]{0,1:T(8,128)}) %all-reduce.4.cloned.1.call-update) | async-done | bytes 262160 | tf_op jit(solution)/shard_map/psum | solution.py:89
  145.7 1.1 copy.44
  146.8 1.0 fusion.20
  147.8 11.7 %cholesky.130 = f32[128,128]{1,0:T(8,128)S(1)} custom-call(f32[128,128]{1,0:T(8,128)S(1)} %cholesky.194), custom_call_target="Cholesky" | custom-call | tf_op jit(solution)/shard_map/jit(cholesky)/cholesky | solution.py:62
  159.6 9.8 %custom-call.14 = f32[1,128,128]{1,2,0:T(8,128)S(1)} custom-call(f32[1,128,128]{2,1,0:T(8,128)S(1)} %get-tuple-element.41), custom_call_target="InvertDiagBlocksLowerTriangular" | custom-call | tf_op jit(solution)/shard_map/jit(cholesky)/cholesky | solution.py:62
  169.9 11.7 %cholesky.147 = f32[128,128]{1,0:T(8,128)S(1)} custom-call(f32[128,128]{1,0:T(8,128)S(1)} %convolution_subtract_fusion.2), custom_call_target="Cholesky" | custom-call | tf_op jit(solution)/shard_map/jit(cholesky)/cholesky | solution.py:62
  184.4 27.4 %all-gather.3.cloned.1.call-done = f32[1024,256]{0,1:T(8,128)} async-done(((f32[256,256]{0,1:T(8,128)}), f32[1024,256]{0,1:T(8,128)}) %all-gather.3.cloned.1.call-update) | async-done | bytes 1048592 | tf_op jit(solution)/shard_map/all_gather | solution.py:90
  211.8 2.6 convolution_bitcast_fusion
  214.6 11.9 %cholesky.164 = f32[128,128]{1,0:T(8,128)S(1)} custom-call(f32[128,128]{1,0:T(8,128)S(1)} %cholesky.197), custom_call_target="Cholesky" | custom-call | tf_op jit(solution)/shard_map/jit(cholesky)/cholesky | solution.py:62
  226.6 9.8 %custom-call.15 = f32[1,128,128]{1,2,0:T(8,128)S(1)} custom-call(f32[1,128,128]{2,1,0:T(8,128)S(1)} %get-tuple-element.37), custom_call_target="InvertDiagBlocksLowerTriangular" | custom-call | tf_op jit(solution)/shard_map/jit(cholesky)/cholesky | solution.py:62
  236.8 11.7 %cholesky.181 = f32[128,128]{1,0:T(8,128)S(1)} custom-call(f32[128,128]{1,0:T(8,128)S(1)} %convolution_subtract_fusion.1), custom_call_target="Cholesky" | custom-call | tf_op jit(solution)/shard_map/jit(cholesky)/cholesky | solution.py:62
  251.3 4.2 %while.1 = (s32[]{:T(128)}, f32[256,256]{1,0:T(8,128)S(1)}, s32[2,2]{1,0:T(2,128)S(1)}, f32[2,128,128]{2,1,0:T(8,128)S(1)}, s32[]{:T(128)}) while((s32[]{:T(128)}, f32[256,256]{1,0:T(8,128)S(1)}, s32[2,2]{1,0:T(2,128)S(1)}, f32[2,128,128]{2,1,0:T(8,128)S(1)}, s32[]{:T(128)}) %tuple.38), condition=%wide.while_cond, body=%wide.while_body.sunk | while | flops 2 | bytes 131189 | solution.py:95
  252.1 1.4 bitcast_dynamic-update-slice_fusion.2
  254.1 1.4 bitcast_dynamic-update-slice_fusion.2
  255.5 19.7 %custom-call.12 = f32[2,128,128]{1,2,0:T(8,128)S(1)} custom-call(f32[2,128,128]{2,1,0:T(8,128)S(1)} %get-tuple-element.10), custom_call_target="InvertDiagBlocksLowerTriangular" | custom-call | tf_op jit(solution)/shard_map/jit(_solve_triangular)/triangular_solve | solution.py:95
  276.1 0.8 copy.48
  276.9 0.8 copy.49
  (64 shorter events, 11.5 us)
Async XLA Ops:
  7.2 138.5 %all-reduce.4.cloned.1.call-start = ((), (), s32[]{:S(2)}) async-start(), calls=%async_computation | async-start | bytes 524288 | tf_op jit(solution)/shard_map/psum | solution.py:89
  8.6 6.7 %collective-permute-start = (bf16[64,3,1,1,128]{4,0,3,2,1:T(8,128)(2,1)S(1)}, bf16[64,3,1,1,128]{4,0,3,2,1:T(8,128)(2,1)S(1)}, u32[]{:S(2)}, u32[]{:S(2)}) collective-permute-start(bf16[64,3,1,1,128]{4,0,3,2,1:T(8,128)(2,1)S(1)} %copy.62), channel_id=1, source_target_pairs={{0,8},{8,16},{16,24},{1,9},{9,17},{17,25},{2,10},{10,18},{18,26},{... | collective-permute-start | bytes 147464 | tf_op jit(solution)/shard_map/ppermute | solution.py:25
  13.6 6.0 %collective-permute-start.1 = (bf16[64,3,1,1,128]{4,0,3,2,1:T(8,128)(2,1)S(1)}, bf16[64,3,1,1,128]{4,0,3,2,1:T(8,128)(2,1)S(1)}, u32[]{:S(2)}, u32[]{:S(2)}) collective-permute-start(bf16[64,3,1,1,128]{4,0,3,2,1:T(8,128)(2,1)S(1)} %copy.63), channel_id=1, source_target_pairs={{8,0},{16,8},{24,16},{9,1},{17,9},{25,17},{10,2},{18,10},{26,18},{... | collective-permute-start | bytes 147464 | tf_op jit(solution)/shard_map/ppermute | solution.py:26
  19.6 5.1 %collective-permute-start.3 = (bf16[64,3,1,10,128]{4,0,3,2,1:T(8,128)(2,1)S(1)}, bf16[64,3,1,10,128]{4,0,3,2,1:T(8,128)(2,1)S(1)}, u32[]{:S(2)}, u32[]{:S(2)}) collective-permute-start(bf16[64,3,1,10,128]{4,0,3,2,1:T(8,128)(2,1)S(1)} %constant_dynamic-update-slice_fusion), channel_id=1, source_target_pairs={{1,0},{2,1},{3,2},{4,3},{5,4},{6,5},{7,6},{9,8},{10,9},{11,10},{12... | collective-permute-start | bytes 1474568 | tf_op jit(solution)/shard_map/ppermute | solution.py:26
  20.9 4.5 %collective-permute-start.2 = (bf16[64,3,1,10,128]{4,0,3,2,1:T(8,128)(2,1)S(1)}, bf16[64,3,1,10,128]{4,0,3,2,1:T(8,128)(2,1)S(1)}, u32[]{:S(2)}, u32[]{:S(2)}) collective-permute-start(bf16[64,3,1,10,128]{4,0,3,2,1:T(8,128)(2,1)S(1)} %constant_dynamic-update-slice_fusion), channel_id=1, source_target_pairs={{0,1},{1,2},{2,3},{3,4},{4,5},{5,6},{6,7},{8,9},{9,10},{10,11},{11... | collective-permute-start | bytes 1474568 | tf_op jit(solution)/shard_map/ppermute | solution.py:25
  26.0 1.0 copy-start
  26.5 1.0 copy-start.2
  28.0 8.9 %collective-permute-start.4 = (f32[1024,256]{1,0:T(8,128)S(1)}, f32[1024,256]{1,0:T(8,128)S(1)}, u32[]{:S(2)}, u32[]{:S(2)}) collective-permute-start(f32[1024,256]{1,0:T(8,128)S(1)} %convolution_multiply_fusion), channel_id=1, source_target_pairs={{0,1},{1,0},{2,3},{3,2},{4,5},{5,4},{6,7},{7,6},{8,9},{9,8},{10,11... | collective-permute-start | bytes 3145736 | tf_op jit(solution)/shard_map/ppermute | solution.py:15
  37.0 30.4 %copy-start.1 = (s32[1,1,256]{2,1,0:T(1,128)S(1)}, s32[1,1,256]{2,1,0:T(1,128)}, u32[]{:S(2)}) copy-start(s32[1,1,256]{2,1,0:T(1,128)} %param.10) | copy-start | bytes 3076
  37.0 26.5 %collective-permute-start.5 = (f32[1024,256]{1,0:T(8,128)S(1)}, f32[1024,256]{1,0:T(8,128)S(1)}, u32[]{:S(2)}, u32[]{:S(2)}) collective-permute-start(f32[1024,256]{1,0:T(8,128)S(1)} %add_select_fusion.1), channel_id=1, source_target_pairs={{0,2},{2,0},{1,3},{3,1},{4,6},{6,4},{5,7},{7,5},{8,10},{10,8},{9,1... | collective-permute-start | bytes 3145736 | tf_op jit(solution)/shard_map/ppermute | solution.py:15
  63.7 26.4 %collective-permute-start.6 = (f32[1024,256]{1,0:T(8,128)S(1)}, f32[1024,256]{1,0:T(8,128)S(1)}, u32[]{:S(2)}, u32[]{:S(2)}) collective-permute-start(f32[1024,256]{1,0:T(8,128)S(1)} %add_select_fusion), channel_id=1, source_target_pairs={{0,4},{4,0},{1,5},{5,1},{2,6},{6,2},{3,7},{7,3},{8,12},{12,8},{9,1... | collective-permute-start | bytes 3145736 | tf_op jit(solution)/shard_map/ppermute | solution.py:15
  92.5 119.3 %all-gather.3.cloned.1.call-start = ((), (), s32[]{:S(2)}) async-start(), calls=%async_computation.1 | async-start | bytes 1310720 | tf_op jit(solution)/shard_map/all_gather | solution.py:90
Sparse Core Ops, SparseCore 0:
  92.6 53.0 all-reduce.3
  184.4 27.2 all-gather.2
where the time goes:
time: 285 us
  waiting for transfers between devices  133 us (47%)
  other arithmetic  92.6 us (32%)
  starting transfers between devices  24 us (8%)
  between operations  17 us (6%)
  local copies, waits for them, and re-layouts  11.4 us (4%)
  matrix products  5.98 us (2%)
    another operation x13, other arithmetic, upper_factor(): return jnp.linalg.cholesky(gram_matrix).T  68.8 us
    psum x1, waiting for transfers between devices, on_device(): block_factor = upper_factor(lax.psum(local_gram, 'mix'))  53 us
    ppermute x3, waiting for transfers between devices, swapped(): return lax.ppermute(block, axis, route)  48.6 us
    all_gather x1, waiting for transfers between devices, on_device(): every_factor = lax.all_gather(block_factor[None], 'row', axis=0, tiled=True)  27.4 us
    another operation x2, other arithmetic, on_device(): solved = jax.scipy.linalg.solve_triangular(factor.T, picked.T, lower=True)  19.7 us
    ppermute x3, starting transfers between devices, swapped(): return lax.ppermute(block, axis, route)  13.2 us
    ppermute x2, starting transfers between devices, padded(): before = lax.ppermute(last, axis, up)  7.99 us
  transfers between devices with their start and end apart: 9, of which 8 were waited for; matrix products, arithmetic and copies ran while one was open for 1% of the time, Pallas kernels for 0%

commit v1 on v0

--- a/solution.py
+++ b/solution.py
@@ -3,6 +3,11 @@
 import jax.numpy as jnp
 from jax import lax
 from jax.sharding import PartitionSpec as P
+
+
+def summed_here(block, axis):
+    parts = lax.all_gather(block, axis)
+    return jnp.sum(parts, axis=0)
 
 
 def swapped(block, axis, distance):
@@ -86,7 +91,7 @@
         )
         / picked_total
     )
-    block_factor = upper_factor(lax.psum(local_gram, "mix"))
+    block_factor = upper_factor(summed_here(local_gram, "mix"))
     every_factor = lax.all_gather(block_factor[None], "row", axis=0, tiled=True)
     stacked_gram = jnp.einsum(
         "bij,bil->jl", every_factor, every_factor, precision=lax.Precision.HIGHEST

time: 285 us -> 260 us (0.912)
  waiting for transfers between devices: 133 us -> 108 us
    psum x1 -> x0, waiting for transfers between devices: 53 us -> none  [on_device(): block_factor = upper_factor(lax.psum(local_gram, 'mix'))]
    all_gather x0 -> x1, waiting for transfers between devices: none -> 27.4 us  [summed_here(): parts = lax.all_gather(block, axis)]
where the time goes in v1:
time: 260 us; the launch traced here: 259 us
  waiting for transfers between devices  108 us (42%)
  other arithmetic  93.4 us (36%)
  starting transfers between devices  24 us (9%)
  between operations  17 us (7%)
  local copies, waits for them, and re-layouts  10.3 us (4%)
  matrix products  6 us (2%)
    another operation x13, other arithmetic, upper_factor(): return jnp.linalg.cholesky(gram_matrix).T  68.8 us
    ppermute x3, waiting for transfers between devices, swapped(): return lax.ppermute(block, axis, route)  48.6 us
    all_gather x1, waiting for transfers between devices, on_device(): every_factor = lax.all_gather(block_factor[None], 'row', axis=0, tiled=True)  28 us
    all_gather x1, waiting for transfers between devices, summed_here(): parts = lax.all_gather(block, axis)  27.4 us
    another operation x2, other arithmetic, on_device(): solved = jax.scipy.linalg.solve_triangular(factor.T, picked.T, lower=True)  19.7 us
    ppermute x3, starting transfers between devices, swapped(): return lax.ppermute(block, axis, route)  13.2 us
    ppermute x2, starting transfers between devices, padded(): before = lax.ppermute(last, axis, up)  7.99 us
  transfers between devices with their start and end apart: 9, of which 8 were waited for; matrix products, arithmetic and copies ran while one was open for 1% of the time, Pallas kernels for 0%

profile of v1, /device:TPU:0, one launch (start us, length us, event | category | flops | bytes accessed | tf_op | source)
XLA Modules:
  0.0 259.4 jit_solution(17922887509486088498)
XLA Ops:
  7.2 1.3 fusion.46
  8.5 4.9 %collective-permute-start = (bf16[64,3,1,1,128]{4,0,3,2,1:T(8,128)(2,1)S(1)}, bf16[64,3,1,1,128]{4,0,3,2,1:T(8,128)(2,1)S(1)}, u32[]{:S(2)}, u32[]{:S(2)}) collective-permute-start(bf16[64,3,1,1,128]{4,0,3,2,1:T(8,128)(2,1)S(1)} %copy.58), channel_id=1, source_target_pairs={{0,8},{8,16},{16,24},{1,9},{9,17},{17,25},{2,10},{10,18},{18,26},{... | collective-permute-start | bytes 147464 | tf_op jit(solution)/shard_map/ppermute | solution.py:30
  13.5 1.3 collective-permute-start.1
  15.2 1.1 constant_dynamic-update-slice_fusion.1
  16.3 3.2 %collective-permute-done.1 = bf16[64,3,1,1,128]{4,0,3,2,1:T(8,128)(2,1)S(1)} collective-permute-done((bf16[64,3,1,1,128]{4,0,3,2,1:T(8,128)(2,1)S(1)}, bf16[64,3,1,1,128]{4,0,3,2,1:T(8,128)(2,1)S(1)}, u32[]{:S(2)}, u32[]{:S(2)}) %collective-permute-start.1) | collective-permute-done | bytes 49184 | tf_op jit(solution)/shard_map/ppermute | solution.py:31
  19.5 1.3 collective-permute-start.3
  20.8 3.1 %collective-permute-start.2 = (bf16[64,3,1,10,128]{4,0,3,2,1:T(8,128)(2,1)S(1)}, bf16[64,3,1,10,128]{4,0,3,2,1:T(8,128)(2,1)S(1)}, u32[]{:S(2)}, u32[]{:S(2)}) collective-permute-start(bf16[64,3,1,10,128]{4,0,3,2,1:T(8,128)(2,1)S(1)} %constant_dynamic-update-slice_fusion), channel_id=1, source_target_pairs={{0,1},{1,2},{2,3},{3,4},{4,5},{5,6},{6,7},{8,9},{9,10},{10,11},{11... | collective-permute-start | bytes 1474568 | tf_op jit(solution)/shard_map/ppermute | solution.py:30
  24.5 0.7 collective-permute-done.2
  27.9 6.6 %collective-permute-start.4 = (f32[1024,256]{1,0:T(8,128)S(1)}, f32[1024,256]{1,0:T(8,128)S(1)}, u32[]{:S(2)}, u32[]{:S(2)}) collective-permute-start(f32[1024,256]{1,0:T(8,128)S(1)} %convolution_multiply_fusion), channel_id=1, source_target_pairs={{0,1},{1,0},{2,3},{3,2},{4,5},{5,4},{6,7},{7,6},{8,9},{9,8},{10,11... | collective-permute-start | bytes 3145736 | tf_op jit(solution)/shard_map/ppermute | solution.py:20
  34.5 2.3 collective-permute-done.4
  36.9 2.8 %collective-permute-start.5 = (f32[1024,256]{1,0:T(8,128)S(1)}, f32[1024,256]{1,0:T(8,128)S(1)}, u32[]{:S(2)}, u32[]{:S(2)}) collective-permute-start(f32[1024,256]{1,0:T(8,128)S(1)} %add_select_fusion.1), channel_id=1, source_target_pairs={{0,2},{2,0},{1,3},{3,1},{4,6},{6,4},{5,7},{7,5},{8,10},{10,8},{9,1... | collective-permute-start | bytes 3145736 | tf_op jit(solution)/shard_map/ppermute | solution.py:20
  39.8 23.7 %collective-permute-done.5 = f32[1024,256]{1,0:T(8,128)S(1)} collective-permute-done((f32[1024,256]{1,0:T(8,128)S(1)}, f32[1024,256]{1,0:T(8,128)S(1)}, u32[]{:S(2)}, u32[]{:S(2)}) %collective-permute-start.5) | collective-permute-done | bytes 1048608 | tf_op jit(solution)/shard_map/ppermute | solution.py:20
  63.6 3.7 %collective-permute-start.6 = (f32[1024,256]{1,0:T(8,128)S(1)}, f32[1024,256]{1,0:T(8,128)S(1)}, u32[]{:S(2)}, u32[]{:S(2)}) collective-permute-start(f32[1024,256]{1,0:T(8,128)S(1)} %add_select_fusion), channel_id=1, source_target_pairs={{0,4},{4,0},{1,5},{5,1},{2,6},{6,2},{3,7},{7,3},{8,12},{12,8},{9,1... | collective-permute-start | bytes 3145736 | tf_op jit(solution)/shard_map/ppermute | solution.py:20
  67.4 22.6 %collective-permute-done.6 = f32[1024,256]{1,0:T(8,128)S(1)} collective-permute-done((f32[1024,256]{1,0:T(8,128)S(1)}, f32[1024,256]{1,0:T(8,128)S(1)}, u32[]{:S(2)}, u32[]{:S(2)}) %collective-permute-start.6) | collective-permute-done | bytes 1048608 | tf_op jit(solution)/shard_map/ppermute | solution.py:20
  90.1 1.0 gather_fusion
  91.2 1.1 convolution_multiply_fusion.1
  92.6 27.4 %all-gather.5.cloned.1.call-done = f32[2048,256]{1,0:T(8,128)} async-done(((f32[256,256]{1,0:T(8,128)}), f32[2048,256]{1,0:T(8,128)}) %all-gather.5.cloned.1.call-update) | async-done | bytes 2097168 | tf_op jit(solution)/shard_map/all_gather | solution.py:9
  120.0 1.8 reduce_sum.9
  121.9 11.7 %cholesky.130 = f32[128,128]{1,0:T(8,128)S(1)} custom-call(f32[128,128]{1,0:T(8,128)S(1)} %cholesky.194), custom_call_target="Cholesky" | custom-call | tf_op jit(solution)/shard_map/jit(cholesky)/cholesky | solution.py:67
  133.7 9.8 %custom-call.14 = f32[1,128,128]{1,2,0:T(8,128)S(1)} custom-call(f32[1,128,128]{2,1,0:T(8,128)S(1)} %get-tuple-element.41), custom_call_target="InvertDiagBlocksLowerTriangular" | custom-call | tf_op jit(solution)/shard_map/jit(cholesky)/cholesky | solution.py:67
  144.0 11.7 %cholesky.147 = f32[128,128]{1,0:T(8,128)S(1)} custom-call(f32[128,128]{1,0:T(8,128)S(1)} %convolution_subtract_fusion.2), custom_call_target="Cholesky" | custom-call | tf_op jit(solution)/shard_map/jit(cholesky)/cholesky | solution.py:67
  158.5 28.0 %all-gather.7.cloned.1.call-done = f32[1024,256]{0,1:T(8,128)} async-done(((f32[256,256]{0,1:T(8,128)}), f32[1024,256]{0,1:T(8,128)}) %all-gather.7.cloned.1.call-update) | async-done | bytes 1048592 | tf_op jit(solution)/shard_map/all_gather | solution.py:95
  186.6 2.6 convolution_bitcast_fusion
  189.3 11.9 %cholesky.164 = f32[128,128]{1,0:T(8,128)S(1)} custom-call(f32[128,128]{1,0:T(8,128)S(1)} %cholesky.197), custom_call_target="Cholesky" | custom-call | tf_op jit(solution)/shard_map/jit(cholesky)/cholesky | solution.py:67
  201.3 9.8 %custom-call.15 = f32[1,128,128]{1,2,0:T(8,128)S(1)} custom-call(f32[1,128,128]{2,1,0:T(8,128)S(1)} %get-tuple-element.37), custom_call_target="InvertDiagBlocksLowerTriangular" | custom-call | tf_op jit(solution)/shard_map/jit(cholesky)/cholesky | solution.py:67
  211.6 11.7 %cholesky.181 = f32[128,128]{1,0:T(8,128)S(1)} custom-call(f32[128,128]{1,0:T(8,128)S(1)} %convolution_subtract_fusion.1), custom_call_target="Cholesky" | custom-call | tf_op jit(solution)/shard_map/jit(cholesky)/cholesky | solution.py:67
  226.0 4.2 %while.1 = (s32[]{:T(128)}, f32[256,256]{1,0:T(8,128)S(1)}, s32[2,2]{1,0:T(2,128)S(1)}, f32[2,128,128]{2,1,0:T(8,128)S(1)}, s32[]{:T(128)}) while((s32[]{:T(128)}, f32[256,256]{1,0:T(8,128)S(1)}, s32[2,2]{1,0:T(2,128)S(1)}, f32[2,128,128]{2,1,0:T(8,128)S(1)}, s32[]{:T(128)}) %tuple.38), condition=%wide.while_cond, body=%wide.while_body.sunk | while | flops 2 | bytes 131189 | solution.py:100
  226.9 1.4 bitcast_dynamic-update-slice_fusion.2
  228.8 1.4 bitcast_dynamic-update-slice_fusion.2
  230.2 19.7 %custom-call.12 = f32[2,128,128]{1,2,0:T(8,128)S(1)} custom-call(f32[2,128,128]{2,1,0:T(8,128)S(1)} %get-tuple-element.10), custom_call_target="InvertDiagBlocksLowerTriangular" | custom-call | tf_op jit(solution)/shard_map/jit(_solve_triangular)/triangular_solve | solution.py:100
  250.8 0.8 copy.45
  251.7 0.8 copy.46
  (65 shorter events, 10.9 us)
Async XLA Ops:
  7.2 112.8 %all-gather.5.cloned.1.call-start = ((), (), s32[]{:S(2)}) async-start(), calls=%async_computation | async-start | bytes 2359296 | tf_op jit(solution)/shard_map/all_gather | solution.py:9
  8.5 6.7 %collective-permute-start = (bf16[64,3,1,1,128]{4,0,3,2,1:T(8,128)(2,1)S(1)}, bf16[64,3,1,1,128]{4,0,3,2,1:T(8,128)(2,1)S(1)}, u32[]{:S(2)}, u32[]{:S(2)}) collective-permute-start(bf16[64,3,1,1,128]{4,0,3,2,1:T(8,128)(2,1)S(1)} %copy.58), channel_id=1, source_target_pairs={{0,8},{8,16},{16,24},{1,9},{9,17},{17,25},{2,10},{10,18},{18,26},{... | collective-permute-start | bytes 147464 | tf_op jit(solution)/shard_map/ppermute | solution.py:30
  13.5 6.0 %collective-permute-start.1 = (bf16[64,3,1,1,128]{4,0,3,2,1:T(8,128)(2,1)S(1)}, bf16[64,3,1,1,128]{4,0,3,2,1:T(8,128)(2,1)S(1)}, u32[]{:S(2)}, u32[]{:S(2)}) collective-permute-start(bf16[64,3,1,1,128]{4,0,3,2,1:T(8,128)(2,1)S(1)} %copy.59), channel_id=1, source_target_pairs={{8,0},{16,8},{24,16},{9,1},{17,9},{25,17},{10,2},{18,10},{26,18},{... | collective-permute-start | bytes 147464 | tf_op jit(solution)/shard_map/ppermute | solution.py:31
  19.5 5.1 %collective-permute-start.3 = (bf16[64,3,1,10,128]{4,0,3,2,1:T(8,128)(2,1)S(1)}, bf16[64,3,1,10,128]{4,0,3,2,1:T(8,128)(2,1)S(1)}, u32[]{:S(2)}, u32[]{:S(2)}) collective-permute-start(bf16[64,3,1,10,128]{4,0,3,2,1:T(8,128)(2,1)S(1)} %constant_dynamic-update-slice_fusion), channel_id=1, source_target_pairs={{1,0},{2,1},{3,2},{4,3},{5,4},{6,5},{7,6},{9,8},{10,9},{11,10},{12... | collective-permute-start | bytes 1474568 | tf_op jit(solution)/shard_map/ppermute | solution.py:31
  20.8 4.5 %collective-permute-start.2 = (bf16[64,3,1,10,128]{4,0,3,2,1:T(8,128)(2,1)S(1)}, bf16[64,3,1,10,128]{4,0,3,2,1:T(8,128)(2,1)S(1)}, u32[]{:S(2)}, u32[]{:S(2)}) collective-permute-start(bf16[64,3,1,10,128]{4,0,3,2,1:T(8,128)(2,1)S(1)} %constant_dynamic-update-slice_fusion), channel_id=1, source_target_pairs={{0,1},{1,2},{2,3},{3,4},{4,5},{5,6},{6,7},{8,9},{9,10},{10,11},{11... | collective-permute-start | bytes 1474568 | tf_op jit(solution)/shard_map/ppermute | solution.py:30
  25.9 1.0 copy-start
  26.4 1.0 copy-start.2
  27.9 8.9 %collective-permute-start.4 = (f32[1024,256]{1,0:T(8,128)S(1)}, f32[1024,256]{1,0:T(8,128)S(1)}, u32[]{:S(2)}, u32[]{:S(2)}) collective-permute-start(f32[1024,256]{1,0:T(8,128)S(1)} %convolution_multiply_fusion), channel_id=1, source_target_pairs={{0,1},{1,0},{2,3},{3,2},{4,5},{5,4},{6,7},{7,6},{8,9},{9,8},{10,11... | collective-permute-start | bytes 3145736 | tf_op jit(solution)/shard_map/ppermute | solution.py:20
  36.9 30.4 %copy-start.1 = (s32[1,1,256]{2,1,0:T(1,128)S(1)}, s32[1,1,256]{2,1,0:T(1,128)}, u32[]{:S(2)}) copy-start(s32[1,1,256]{2,1,0:T(1,128)} %param.10) | copy-start | bytes 3076
  36.9 26.5 %collective-permute-start.5 = (f32[1024,256]{1,0:T(8,128)S(1)}, f32[1024,256]{1,0:T(8,128)S(1)}, u32[]{:S(2)}, u32[]{:S(2)}) collective-permute-start(f32[1024,256]{1,0:T(8,128)S(1)} %add_select_fusion.1), channel_id=1, source_target_pairs={{0,2},{2,0},{1,3},{3,1},{4,6},{6,4},{5,7},{7,5},{8,10},{10,8},{9,1... | collective-permute-start | bytes 3145736 | tf_op jit(solution)/shard_map/ppermute | solution.py:20
  63.6 26.4 %collective-permute-start.6 = (f32[1024,256]{1,0:T(8,128)S(1)}, f32[1024,256]{1,0:T(8,128)S(1)}, u32[]{:S(2)}, u32[]{:S(2)}) collective-permute-start(f32[1024,256]{1,0:T(8,128)S(1)} %add_select_fusion), channel_id=1, source_target_pairs={{0,4},{4,0},{1,5},{5,1},{2,6},{6,2},{3,7},{7,3},{8,12},{12,8},{9,1... | collective-permute-start | bytes 3145736 | tf_op jit(solution)/shard_map/ppermute | solution.py:20
  92.4 94.2 %all-gather.7.cloned.1.call-start = ((), (), s32[]{:S(2)}) async-start(), calls=%async_computation.1 | async-start | bytes 1310720 | tf_op jit(solution)/shard_map/all_gather | solution.py:95
Sparse Core Ops, SparseCore 0:
  92.5 27.4 all-gather.4
  158.6 27.9 all-gather.6
